TPU v7x, 32 devices: a whole 2x2x4 slice. The times are simulated.
32 devices in a mesh: fsdp: 8 (over y, x, core), seq: 4 (over z).
Axes of the slice: x: 2, y: 2, z: 4, core: 2. Of those that a mesh axis runs over, the one named last changes fastest.
Arguments:
- inputs: bfloat16 [24, 320, 1024], P('fsdp', 'seq'), may hold values from -6 to 6
- lengths: int32 [24], P('fsdp'), may hold values from 256 to 320, as said below
- cotangent: bfloat16 [24, 320, 1024], P('fsdp', 'seq'), may hold values from -6 to 6
- attn_gain: bfloat16 [1024], P('fsdp'), may hold values from 0.25 to 1.75
- attn_shift: bfloat16 [1024], P('fsdp'), may hold values from -1 to 1
- qkv_weight: bfloat16 [1024, 3072], P('fsdp'), may hold values from -0.1875 to 0.1875
- qv_bias: bfloat16 [2048], P('fsdp'), may hold values from -0.5 to 0.5
- proj_weight: bfloat16 [1024, 1024], P('fsdp'), may hold values from -1.5 to 1.5
- proj_bias: bfloat16 [1024], P('fsdp'), may hold values from -1 to 1
- mlp_gain: bfloat16 [1024], P('fsdp'), may hold values from 0.25 to 1.75
- mlp_shift: bfloat16 [1024], P('fsdp'), may hold values from -1 to 1
- up_weight: bfloat16 [1024, 4096], P('fsdp'), may hold values from -0.1875 to 0.1875
- up_bias: bfloat16 [4096], P('fsdp'), may hold values from -1 to 1
- down_weight: bfloat16 [4096, 1024], P('fsdp'), may hold values from -0.09375 to 0.09375
- down_bias: bfloat16 [1024], P('fsdp'), may hold values from -1 to 1
Outputs:
- output: bfloat16 [24, 320, 1024], P('fsdp', 'seq')
- input_grad: bfloat16 [24, 320, 1024], P('fsdp', 'seq')
- attn_gain_grad: float32 [1024], P('fsdp')
- attn_shift_grad: float32 [1024], P('fsdp')
- query_key_value_weight_gradient: float32 [1024, 3072], P('fsdp')
- qv_bias_grad: float32 [2048], P('fsdp')
- proj_weight_grad: float32 [1024, 1024], P('fsdp')
- proj_bias_grad: float32 [1024], P('fsdp')
- mlp_gain_grad: float32 [1024], P('fsdp')
- mlp_shift_grad: float32 [1024], P('fsdp')
- up_weight_grad: float32 [1024, 4096], P('fsdp')
- up_bias_grad: float32 [4096], P('fsdp')
- down_weight_grad: float32 [4096, 1024], P('fsdp')
- down_bias_grad: float32 [1024], P('fsdp')
Inputs may be any that keep to these rules, and one draw needn't show every extreme that they name: `lengths`: valid slots of each sequence; slots at or past it are padding; some sequence is full and some has the fewest.
All inputs are finite; a program needn't handle non-finite values.
Results may differ from a plain program's by a relative error of at most 0.015.
Values may be sent and summed in bfloat16 or wider, within the bound.
No kernel may reach another device: no remote copies, remote signals or barrier semaphores. Data moves between devices by JAX's collectives and lax.ppermute only.
A program may use at most 192 MiB of HBM per device.

v0:
```python
import jax
import jax.numpy as jnp
from jax import lax
from jax.sharding import PartitionSpec as P

HEAD = 64
EPSILON = 1e-06
MASKED = -1e30


def layer_norm(value_entries, norm_gain, norm_shift):
    center = value_entries - jnp.mean(value_entries, axis=-1, keepdims=True)
    inverse = lax.rsqrt(jnp.mean(center * center, axis=-1, keepdims=True) + EPSILON)
    normed = center * inverse
    return (normed * norm_gain + norm_shift, normed, inverse)


def norm_back(upstream, normed, inverse, norm_gain):
    scaled = upstream * norm_gain
    return inverse * (
        scaled
        - jnp.mean(scaled, axis=-1, keepdims=True)
        - normed * jnp.mean(scaled * normed, axis=-1, keepdims=True)
    )


def matrix_product(form, left, right):
    return jnp.einsum(form, left, right, preferred_element_type=jnp.float32)


def masked_scores(queries, key_rows, key_valid):
    raw_scores = matrix_product("sqhe,skhe->shqk", queries, key_rows) * HEAD ** (-0.5)
    return jnp.where(key_valid[:, None, None, :], raw_scores, MASKED)


def column_sums(value_entries):
    return jnp.sum(value_entries, axis=(0, 1), dtype=jnp.float32)


def unpack(gathered):
    return tuple(
        (member.astype(jnp.float32) if member.ndim == 1 else member for member in gathered)
    )


def per_device(
    inputs,
    lengths,
    cotangent,
    attn_gain,
    attn_shift,
    qkv_weight,
    qv_bias,
    proj_weight,
    proj_bias,
    mlp_gain,
    mlp_shift,
    up_weight,
    up_bias,
    down_weight,
    down_bias,
):
    seq_count, local_slots, model_width = inputs.shape
    groups_seq = lax.axis_size("seq")
    all_slots = local_slots * groups_seq
    head_width = model_width // groups_seq
    head_count = head_width // HEAD
    slot_start = lax.axis_index("seq") * local_slots
    positions = slot_start + jnp.arange(local_slots, dtype=jnp.int32)
    row_valid_mask = (positions[None, :] < lengths[:, None]).astype(jnp.float32)[:, :, None]
    key_valid = jnp.arange(all_slots, dtype=jnp.int32)[None, :] < lengths[:, None]
    shards = (
        attn_gain,
        attn_shift,
        qkv_weight,
        qv_bias,
        proj_weight,
        proj_bias,
        mlp_gain,
        mlp_shift,
        up_weight,
        up_bias,
        down_weight,
        down_bias,
    )
    (
        gain_attn,
        shift_attn,
        query_key_value_weight,
        bias_qv,
        output_projection_weight,
        output_projection_bias,
        gain_mlp,
        shift_mlp,
        up_projection_weight,
        up_projection_bias,
        down_projection_weight,
        down_projection_bias,
    ) = unpack(
        (
            lax.all_gather(shards[0], "fsdp", axis=0, tiled=True),
            lax.all_gather(shards[1], "fsdp", axis=0, tiled=True),
            lax.all_gather(shards[2], "fsdp", axis=0, tiled=True),
            lax.all_gather(shards[3], "fsdp", axis=0, tiled=True),
            lax.all_gather(shards[4], "fsdp", axis=0, tiled=True),
            lax.all_gather(shards[5], "fsdp", axis=0, tiled=True),
            lax.all_gather(shards[6], "fsdp", axis=0, tiled=True),
            lax.all_gather(shards[7], "fsdp", axis=0, tiled=True),
            lax.all_gather(shards[8], "fsdp", axis=0, tiled=True),
            lax.all_gather(shards[9], "fsdp", axis=0, tiled=True),
            lax.all_gather(shards[10], "fsdp", axis=0, tiled=True),
            lax.all_gather(shards[11], "fsdp", axis=0, tiled=True),
        )
    )
    value_entries = inputs.astype(jnp.float32)
    normed_attn, unit_attn, inverse_attn = layer_norm(value_entries, gain_attn, shift_attn)
    normalized_reduced = normed_attn.astype(jnp.bfloat16)
    complete_bias = jnp.concatenate(
        [bias_qv[:model_width], jnp.zeros((model_width,), jnp.float32), bias_qv[model_width:]]
    )
    query_key_value_rows = (
        matrix_product("vgp,pf->vgf", normalized_reduced, query_key_value_weight) + complete_bias
    ).astype(jnp.bfloat16)
    query_key_value_rows = query_key_value_rows.reshape(seq_count, local_slots, 3, model_width)
    heads = lax.all_to_all(query_key_value_rows, "seq", split_axis=3, concat_axis=1, tiled=True)
    queries = heads[:, :, 0].reshape(seq_count, all_slots, head_count, HEAD)
    key_rows = heads[:, :, 1].reshape(seq_count, all_slots, head_count, HEAD)
    value_rows = heads[:, :, 2].reshape(seq_count, all_slots, head_count, HEAD)
    scores = masked_scores(queries, key_rows, key_valid)
    row_max = jnp.max(scores, axis=-1, keepdims=True)
    exponent = jnp.exp(scores - row_max)
    totals = jnp.sum(exponent, axis=-1, keepdims=True)
    probs = exponent / totals
    log_total = row_max + jnp.log(totals)
    context = matrix_product("shqk,skhe->sqhe", probs.astype(jnp.bfloat16), value_rows).astype(
        jnp.bfloat16
    )
    context = context.reshape(seq_count, all_slots, head_width)
    context_row_values = lax.all_to_all(context, "seq", split_axis=1, concat_axis=2, tiled=True)
    hidden_activations = (
        value_entries
        + matrix_product("vgp,pf->vgf", context_row_values, output_projection_weight)
        + output_projection_bias
    )
    normed_mlp, unit_mlp, inverse_mlp = layer_norm(hidden_activations, gain_mlp, shift_mlp)
    normalized_feedforward_reduced = normed_mlp.astype(jnp.bfloat16)
    preactivation_values = (
        matrix_product("bux,xa->bua", normalized_feedforward_reduced, up_projection_weight)
        + up_projection_bias
    )
    activation_reduced = jax.nn.gelu(preactivation_values).astype(jnp.bfloat16)
    output = (
        row_valid_mask
        * (
            hidden_activations
            + matrix_product("ohq,qt->oht", activation_reduced, down_projection_weight)
            + down_projection_bias
        )
    ).astype(jnp.bfloat16)
    (
        gain_attn,
        shift_attn,
        query_key_value_weight,
        bias_qv,
        output_projection_weight,
        output_projection_bias,
        gain_mlp,
        shift_mlp,
        up_projection_weight,
        up_projection_bias,
        down_projection_weight,
        down_projection_bias,
    ) = unpack(
        (
            lax.all_gather(shards[0], "fsdp", axis=0, tiled=True),
            lax.all_gather(shards[1], "fsdp", axis=0, tiled=True),
            lax.all_gather(shards[2], "fsdp", axis=0, tiled=True),
            lax.all_gather(shards[3], "fsdp", axis=0, tiled=True),
            lax.all_gather(shards[4], "fsdp", axis=0, tiled=True),
            lax.all_gather(shards[5], "fsdp", axis=0, tiled=True),
            lax.all_gather(shards[6], "fsdp", axis=0, tiled=True),
            lax.all_gather(shards[7], "fsdp", axis=0, tiled=True),
            lax.all_gather(shards[8], "fsdp", axis=0, tiled=True),
            lax.all_gather(shards[9], "fsdp", axis=0, tiled=True),
            lax.all_gather(shards[10], "fsdp", axis=0, tiled=True),
            lax.all_gather(shards[11], "fsdp", axis=0, tiled=True),
        )
    )
    upstream = cotangent.astype(jnp.float32) * row_valid_mask
    incoming_reduced = upstream.astype(jnp.bfloat16)
    down_gradient = matrix_product("zmx,zma->xa", activation_reduced, incoming_reduced)
    down_bias_grad = column_sums(upstream)
    activation_gradient = matrix_product("jeo,xo->jex", incoming_reduced, down_projection_weight)
    preactivation_gradient = jax.vjp(jax.nn.gelu, preactivation_values)[1](activation_gradient)[
        0
    ].astype(jnp.bfloat16)
    up_projection_gradient = matrix_product(
        "znb,zng->bg", normalized_feedforward_reduced, preactivation_gradient
    )
    up_bias_grad = column_sums(preactivation_gradient)
    normalized_gradient = matrix_product(
        "ikh,th->ikt", preactivation_gradient, up_projection_weight
    )
    mlp_gain_grad = column_sums(normalized_gradient * unit_mlp)
    mlp_shift_grad = column_sums(normalized_gradient)
    hidden_grad = upstream + norm_back(normalized_gradient, unit_mlp, inverse_mlp, gain_mlp)
    attention_gradient = hidden_grad.astype(jnp.bfloat16)
    proj_bias_grad = column_sums(attention_gradient)
    projection_gradient = matrix_product("ftk,ftj->kj", context_row_values, attention_gradient)
    context_gradient = matrix_product(
        "fgo,xo->fgx", attention_gradient, output_projection_weight
    ).astype(jnp.bfloat16)
    head_grad = lax.all_to_all(context_gradient, "seq", split_axis=2, concat_axis=1, tiled=True)
    head_grad = head_grad.reshape(seq_count, all_slots, head_count, HEAD)
    scores = masked_scores(queries, key_rows, key_valid)
    probs = jnp.exp(scores - log_total)
    probs_grad = matrix_product("sqhe,skhe->shqk", head_grad, value_rows)
    inner = jnp.sum(probs * probs_grad, axis=-1, keepdims=True)
    scores_grad = (probs * (probs_grad - inner) * HEAD ** (-0.5)).astype(jnp.bfloat16)
    query_grad = matrix_product("shqk,skhe->sqhe", scores_grad, key_rows)
    key_grad = matrix_product("shqk,sqhe->skhe", scores_grad, queries)
    value_grad = matrix_product("shqk,sqhe->skhe", probs.astype(jnp.bfloat16), head_grad)
    stacked = jnp.stack([query_grad, key_grad, value_grad], axis=2).astype(jnp.bfloat16)
    stacked = stacked.reshape(seq_count, all_slots, 3, head_width)
    query_key_value_gradient = lax.all_to_all(
        stacked, "seq", split_axis=1, concat_axis=3, tiled=True
    )
    query_key_value_gradient = query_key_value_gradient.reshape(
        seq_count, local_slots, 3 * model_width
    )
    query_key_value_weight_gradient = matrix_product(
        "ftk,ftj->kj", normalized_reduced, query_key_value_gradient
    )
    qkv_sums = column_sums(query_key_value_gradient)
    qv_bias_grad = jnp.concatenate([qkv_sums[:model_width], qkv_sums[2 * model_width :]])
    attention_normed_gradient = matrix_product(
        "fgo,xo->fgx", query_key_value_gradient, query_key_value_weight
    )
    attn_gain_grad = column_sums(attention_normed_gradient * unit_attn)
    attn_shift_grad = column_sums(attention_normed_gradient)
    input_grad = (
        hidden_grad + norm_back(attention_normed_gradient, unit_attn, inverse_attn, gain_attn)
    ).astype(jnp.bfloat16)
    shares = (
        lax.psum_scatter(attn_gain_grad, "fsdp", scatter_dimension=0, tiled=True),
        lax.psum_scatter(attn_shift_grad, "fsdp", scatter_dimension=0, tiled=True),
        lax.psum_scatter(query_key_value_weight_gradient, "fsdp", scatter_dimension=0, tiled=True),
        lax.psum_scatter(qv_bias_grad, "fsdp", scatter_dimension=0, tiled=True),
        lax.psum_scatter(projection_gradient, "fsdp", scatter_dimension=0, tiled=True),
        lax.psum_scatter(proj_bias_grad, "fsdp", scatter_dimension=0, tiled=True),
        lax.psum_scatter(mlp_gain_grad, "fsdp", scatter_dimension=0, tiled=True),
        lax.psum_scatter(mlp_shift_grad, "fsdp", scatter_dimension=0, tiled=True),
        lax.psum_scatter(up_projection_gradient, "fsdp", scatter_dimension=0, tiled=True),
        lax.psum_scatter(up_bias_grad, "fsdp", scatter_dimension=0, tiled=True),
        lax.psum_scatter(down_gradient, "fsdp", scatter_dimension=0, tiled=True),
        lax.psum_scatter(down_bias_grad, "fsdp", scatter_dimension=0, tiled=True),
    )
    summed = tuple(
        (
            lax.psum(shares[0].astype(jnp.bfloat16), "seq").astype(jnp.float32),
            lax.psum(shares[1].astype(jnp.bfloat16), "seq").astype(jnp.float32),
            lax.psum(shares[2].astype(jnp.bfloat16), "seq").astype(jnp.float32),
            lax.psum(shares[3].astype(jnp.bfloat16), "seq").astype(jnp.float32),
            lax.psum(shares[4].astype(jnp.bfloat16), "seq").astype(jnp.float32),
            lax.psum(shares[5].astype(jnp.bfloat16), "seq").astype(jnp.float32),
            lax.psum(shares[6].astype(jnp.bfloat16), "seq").astype(jnp.float32),
            lax.psum(shares[7].astype(jnp.bfloat16), "seq").astype(jnp.float32),
            lax.psum(shares[8].astype(jnp.bfloat16), "seq").astype(jnp.float32),
            lax.psum(shares[9].astype(jnp.bfloat16), "seq").astype(jnp.float32),
            lax.psum(shares[10].astype(jnp.bfloat16), "seq").astype(jnp.float32),
            lax.psum(shares[11].astype(jnp.bfloat16), "seq").astype(jnp.float32),
        )
    )
    return (output, input_grad) + summed


def solution(mesh):
    in_specs = (
        P("fsdp", "seq", None),
        P("fsdp"),
        P("fsdp", "seq", None),
        P("fsdp"),
        P("fsdp"),
        P("fsdp", None),
        P("fsdp"),
        P("fsdp", None),
        P("fsdp"),
        P("fsdp"),
        P("fsdp"),
        P("fsdp", None),
        P("fsdp"),
        P("fsdp", None),
        P("fsdp"),
    )
    out_specs = (
        P("fsdp", "seq", None),
        P("fsdp", "seq", None),
        P("fsdp"),
        P("fsdp"),
        P("fsdp", None),
        P("fsdp"),
        P("fsdp", None),
        P("fsdp"),
        P("fsdp"),
        P("fsdp"),
        P("fsdp", None),
        P("fsdp"),
        P("fsdp", None),
        P("fsdp"),
    )
    return jax.shard_map(
        per_device, mesh=mesh, in_specs=in_specs, out_specs=out_specs, check_vma=False
    )
```

profile of v0, /device:TPU:0, one launch (start us, length us, event | category | flops | bytes accessed | tf_op | source)
XLA Modules:
  0.0 826.4 jit_solution(11115464629321847686)
XLA Ops:
  10.6 10.3 %all-gather = bf16[8,1,128]{2,1,0:T(2,128)(2,1)S(1)} all-gather(bf16[1,1,128]{2,1,0:T(2,128)(2,1)} %bitcast.172), channel_id=1, replica_groups=mesh['fsdp'=8,'seq'=4] {'fsdp'}, dimensions={0}, use_global_device_ids=true | all-gather | bytes 2304 | tf_op jit(solution)/shard_map/all_gather | solution.py:101
  20.9 8.6 %all-gather.1 = bf16[8,1,128]{2,1,0:T(2,128)(2,1)S(1)} all-gather(bf16[1,1,128]{2,1,0:T(2,128)(2,1)} %bitcast.173), channel_id=1, replica_groups=mesh['fsdp'=8,'seq'=4] {'fsdp'}, dimensions={0}, use_global_device_ids=true | all-gather | bytes 2304 | tf_op jit(solution)/shard_map/all_gather | solution.py:102
  39.1 19.0 %all-gather.13.cloned.1.call-done = bf16[1024,3072]{1,0:T(8,128)(2,1)} async-done(((bf16[128,3072]{1,0:T(8,128)(2,1)}), bf16[1024,3072]{1,0:T(8,128)(2,1)}) %all-gather.13.cloned.1.call-update) | async-done | bytes 6291472 | tf_op jit(solution)/shard_map/all_gather | solution.py:103
  81.6 35.3 %all-to-all-done = bf16[4,2,92160]{2,1,0:T(2,128)(2,1)} async-done(((bf16[4,2,92160]{2,1,0:T(2,128)(2,1)}), bf16[4,2,92160]{2,1,0:T(2,128)(2,1)}, u32[]{:S(2)}, u32[]{:S(2)}) %all-to-all-start) | async-done | bytes 1474592 | tf_op jit(solution)/shard_map/all_to_all | solution.py:125
  137.9 8.6 %all-gather.3 = bf16[8,1,128]{2,1,0:T(2,128)(2,1)S(1)} all-gather(bf16[1,1,128]{2,1,0:T(2,128)(2,1)S(1)} %bitcast.174), channel_id=1, replica_groups=mesh['fsdp'=8,'seq'=4] {'fsdp'}, dimensions={0}, use_global_device_ids=true | all-gather | bytes 2304 | tf_op jit(solution)/shard_map/all_gather | solution.py:106
  154.4 8.6 %all-gather.5 = bf16[8,1,128]{2,1,0:T(2,128)(2,1)S(1)} all-gather(bf16[1,1,128]{2,1,0:T(2,128)(2,1)S(1)} %bitcast.176), channel_id=1, replica_groups=mesh['fsdp'=8,'seq'=4] {'fsdp'}, dimensions={0}, use_global_device_ids=true | all-gather | bytes 2304 | tf_op jit(solution)/shard_map/all_gather | solution.py:108
  163.0 8.2 all-gather.6
  174.2 8.0 fusion.15
  182.2 18.3 %all-gather.19.cloned.1.call-done = bf16[4096,1024]{1,0:T(8,128)(2,1)} async-done(((bf16[512,1024]{1,0:T(8,128)(2,1)}), bf16[4096,1024]{1,0:T(8,128)(2,1)}) %all-gather.19.cloned.1.call-update) | async-done | bytes 8388624 | tf_op jit(solution)/shard_map/all_gather | solution.py:111
  200.5 11.3 %convert_reduce_fusion = (f32[4096]{0:T(1024)S(1)}, bf16[3,80,4096]{2,1,0:T(8,128)(2,1)S(1)}) fusion(f32[3,80,4096]{2,1,0:T(8,128)} %fusion.15, bf16[4096,1024]{1,0:T(8,128)(2,1)} %all-gather.19.cloned.1.call-done, bf16[3,80,1024]{2,1,0:T(8,128)(2,1)S(1)} %copy-done.13, f32[3,80]{1,0:T(4,128)S(1)} %compare_convert_fusion), kind=kOutput, calls=%fused_computation.35 | convolution fusion | flops 2035625984 | bytes 14795712 | tf_op jit(solution)/shard_map/jeo,xo->jex/dot_general | solution.py:28
  229.8 14.1 %all-to-all-done.2 = bf16[4,2,30720]{2,1,0:T(2,128)(2,1)} async-done(((bf16[4,2,30720]{2,1,0:T(2,128)(2,1)}), bf16[4,2,30720]{2,1,0:T(2,128)(2,1)}, u32[]{:S(2)}, u32[]{:S(2)}) %all-to-all-start.2) | async-done | bytes 491552 | tf_op jit(solution)/shard_map/all_to_all | solution.py:213
  260.1 10.5 %fusion.65 = bf16[3,4,64,320]{3,2,1,0:T(8,128)(2,1)S(1)} fusion(bf16[3,320,4,64]{1,3,2,0:T(8,128)(2,1)S(1)} %bitcast.143, f32[3,4,320,320]{2,3,1,0:T(8,128)} %fusion.117, f32[3,4,320,320]{2,3,1,0:T(8,128)} %copy-done, f32[3,4,320]{2,1,0:T(4,128)S(1)} %log_add_fusion), kind=kOutput, calls=%fused_computation.61 | convolution fusion | flops 166137920 | bytes 10828800 | tf_op jit(solution)/shard_map/shqk,skhe->sqhe/dot_general | solution.py:28
  272.7 11.4 %fusion.68 = bf16[3,4,64,320]{3,2,1,0:T(8,128)(2,1)} fusion(bf16[3,320,4,64]{1,3,2,0:T(8,128)(2,1)} %bitcast.141, f32[3,4,320,320]{2,3,1,0:T(8,128)} %fusion.117, f32[3,4,320,320]{2,3,1,0:T(8,128)} %copy-done, f32[3,4,320]{2,1,0:T(4,128)S(1)} %log_add_fusion), kind=kOutput, calls=%fused_computation.62 | convolution fusion | flops 166137920 | bytes 10828800 | tf_op jit(solution)/shard_map/shqk,sqhe->skhe/dot_general | solution.py:28
  291.7 48.1 %all_to_all.66 = bf16[3,320,3,256]{3,2,0,1:T(4,128)(2,1)S(1)} all-to-all(bf16[3,320,3,256]{3,2,0,1:T(4,128)(2,1)S(1)} %pad_maximum_fusion), channel_id=1, replica_groups=mesh['fsdp'=8,'seq'=4] {'seq'}, dimensions={1} | all-to-all | bytes 2949120 | tf_op jit(solution)/shard_map/all_to_all | solution.py:225
  353.9 14.7 %convolution_bitcast_fusion = f32[4096,1024]{1,0:T(8,128)} fusion(bf16[3,80,1024]{2,1,0:T(8,128)(2,1)} %param.17, f32[3,80]{1,0:T(4,128)S(1)} %compare_convert_fusion, f32[3,80,4096]{2,1,0:T(8,128)} %fusion.15), kind=kOutput, calls=%fused_computation.1 | convolution fusion | flops 2022850560 | bytes 21201856 | tf_op jit(solution)/shard_map/zmx,zma->xa/dot_general | solution.py:28
  368.7 10.2 %convolution_bitcast_fusion.1 = f32[1024,4096]{1,0:T(8,128)} fusion(bf16[3,80,4096]{2,1,0:T(8,128)(2,1)} %copy-done.11, f32[3,80,1024]{2,1,0:T(8,128)S(1)} %get-tuple-element.55, f32[1024]{0:T(1024)S(1)} %bitcast.158, f32[1024]{0:T(1024)S(1)} %bitcast.156, f32[3,80]{1,0:T(4,128)S(1)} %add_rsqrt_fusion, f32[3,80]{1,0:T(4,128)S(1)} %broadcast_multiply_fusion.4), kind=kOutput, calls=%fused_computation.2 | convolution fusion | flops 2014494720 | bytes 19736448 | tf_op jit(solution)/shard_map/znb,zng->bg/dot_general | solution.py:28
  380.8 63.7 %reduce-scatter.5.cloned.1.call-done = f32[128,3072]{1,0:T(8,128)} async-done(((f32[1024,3072]{1,0:T(8,128)}), f32[128,3072]{1,0:T(8,128)}) %reduce-scatter.5.cloned.1.call-update) | async-done | bytes 1572880 | tf_op jit(solution)/shard_map/reduce_scatter | solution.py:247
  446.9 117.6 %reduce-scatter.11.cloned.1.call-done = f32[512,1024]{1,0:T(8,128)} async-done(((f32[4096,1024]{1,0:T(8,128)}), f32[512,1024]{1,0:T(8,128)}) %reduce-scatter.11.cloned.1.call-update) | async-done | bytes 2097168 | tf_op jit(solution)/shard_map/reduce_scatter | solution.py:255
  567.2 117.2 %reduce-scatter.9.cloned.1.call-done = f32[128,4096]{1,0:T(8,128)} async-done(((f32[1024,4096]{1,0:T(8,128)}), f32[128,4096]{1,0:T(8,128)}) %reduce-scatter.9.cloned.1.call-update) | async-done | bytes 2097168 | tf_op jit(solution)/shard_map/reduce_scatter | solution.py:253
  689.7 8.8 %all-gather.7 = bf16[8,1,128]{2,1,0:T(2,128)(2,1)S(1)} all-gather(bf16[1,1,128]{2,1,0:T(2,128)(2,1)S(1)} %bitcast.177), channel_id=1, replica_groups=mesh['fsdp'=8,'seq'=4] {'fsdp'}, dimensions={0}, use_global_device_ids=true | all-gather | bytes 2304 | tf_op jit(solution)/shard_map/all_gather | solution.py:112
  698.5 8.1 fusion.80
  712.0 25.7 %all-reduce.8 = (bf16[1024]{0:T(1024)(128)(2,1)S(1)}, bf16[1024]{0:T(1024)(128)(2,1)S(1)}, bf16[2048]{0:T(1024)(128)(2,1)S(1)}, bf16[1024]{0:T(1024)(128)(2,1)S(...) all-reduce(f32[1024]{0:T(1024)S(1)} %get-tuple-element.16, ...), channel_id=2, replica_groups=mesh['fsdp'=8,'seq'=4] {'fsdp'}, use_global_device_ids=true, to_apply=%region_12.13.clone | all-reduce | flops 12288 | bytes 73728
  738.3 12.4 %all-reduce.9 = (bf16[128]{0:T(256)(128)(2,1)S(1)}, bf16[128]{0:T(256)(128)(2,1)S(1)}, bf16[256]{0:T(256)(128)(2,1)S(1)}, bf16[128]{0:T(256)(128)(2,1)S(1)}, bf1...) all-reduce(bf16[128]{0:T(256)(128)(2,1)S(1)} %dynamic-slice.31, ...), channel_id=1, replica_groups=mesh['fsdp'=8,'seq'=4] {'seq'}, use_global_device_ids=true, to_apply=%region_13.14 | all-reduce | flops 1536 | bytes 6144 | tf_op jit(solution)/shard_map/psum | solution.py:260
  756.0 55.0 %all-reduce.13.cloned.1.call-done = (bf16[128,3072]{1,0:T(8,128)(2,1)}, bf16[128,1024]{1,0:T(8,128)(2,1)}, bf16[128,4096]{1,0:T(8,128)(2,1)}, bf16[512,1024]{1,0:T(8,128)(2,1)}) async-done(((bf16[128,3072]{1,0:T(8,128)(2,1)}, bf16[128,1024]{1,0:T(8,128)(2,1)}, bf16[128,4096]{1,0:T(8,128)(2,1)}, bf16[512,1024]{1,0:T(8,128)(2,1)}), (bf16[128,3072]{1,0:T(8,128)(2,1)}, bf16[128,1024]{1,0:T(8,128)(2,1)}, ...) | async-done | bytes 3145744 | tf_op jit(solution)/shard_map/psum | solution.py:262
  (165 shorter events, 156.0 us)
Async XLA Ops:
  7.2 31.7 %copy-start.1 = (bf16[3,80,1024]{2,1,0:T(8,128)(2,1)S(1)}, bf16[3,80,1024]{2,1,0:T(8,128)(2,1)}, u32[]{:S(2)}) copy-start(bf16[3,80,1024]{2,1,0:T(8,128)(2,1)} %param.15) | copy-start | bytes 1474564
  7.2 51.0 %all-gather.13.cloned.1.call-start = ((), (), s32[]{:S(2)}) async-start(), calls=%async_computation.8 | async-start | bytes 7077888 | tf_op jit(solution)/shard_map/all_gather | solution.py:103
  7.9 163.5 %all-gather.15.cloned.1.call-start = ((), (), s32[]{:S(2)}) async-start(), calls=%async_computation.9 | async-start | bytes 2359296 | tf_op jit(solution)/shard_map/all_gather | solution.py:105
  8.7 165.5 %all-gather.17.cloned.1.call-start = ((), (), s32[]{:S(2)}) async-start(), calls=%async_computation.10 | async-start | bytes 9437184 | tf_op jit(solution)/shard_map/all_gather | solution.py:109
  9.4 191.1 %all-gather.19.cloned.1.call-start = ((), (), s32[]{:S(2)}) async-start(), calls=%async_computation.11 | async-start | bytes 9437184 | tf_op jit(solution)/shard_map/all_gather | solution.py:111
  71.9 9.7 %copy-start.14 = (s32[3]{0:T(128)S(1)}, s32[3]{0:T(128)}, u32[]{:S(2)}) copy-start(s32[3]{0:T(128)} %param.16) | copy-start | bytes 40
  76.9 40.0 %all-to-all-start = ((bf16[4,2,92160]{2,1,0:T(2,128)(2,1)}), bf16[4,2,92160]{2,1,0:T(2,128)(2,1)}, u32[]{:S(2)}, u32[]{:S(2)}) async-start(bf16[4,2,92160]{2,1,0:T(2,128)(2,1)} %reshape.208), calls=%async_computation | async-start | bytes 2949120 | tf_op jit(solution)/shard_map/all_to_all | solution.py:125
  131.4 15.1 %copy-start.17 = (bf16[128]{0:T(256)(128)(2,1)S(1)}, bf16[128]{0:T(256)(128)(2,1)}, u32[]{:S(2)}) copy-start(bf16[128]{0:T(256)(128)(2,1)} %param.24) | copy-start | bytes 772
  131.4 22.9 %copy-start.18 = (bf16[128]{0:T(256)(128)(2,1)S(1)}, bf16[128]{0:T(256)(128)(2,1)}, u32[]{:S(2)}) copy-start(bf16[128]{0:T(256)(128)(2,1)} %param.25) | copy-start | bytes 772
  133.1 38.4 %copy-start.2 = (bf16[3,80,1024]{2,1,0:T(8,128)(2,1)S(1)}, bf16[3,80,1024]{2,1,0:T(8,128)(2,1)}, u32[]{:S(2)}) copy-start(bf16[3,80,1024]{2,1,0:T(8,128)(2,1)} %param.15) | copy-start | bytes 1474564
  134.3 37.0 %all-to-all-start.1 = ((bf16[3,320,256]{2,0,1:T(4,128)(2,1)}), bf16[3,320,256]{2,0,1:T(4,128)(2,1)S(1)}, u32[]{:S(2)}, u32[]{:S(2)}) async-start(bf16[3,320,256]{2,0,1:T(4,128)(2,1)} %copy.80), calls=%async_computation.1 | async-start | bytes 1310720 | tf_op jit(solution)/shard_map/all_to_all | solution.py:139
  137.8 241.2 %reduce-scatter.7.cloned.1.call-start = ((), (), s32[]{:S(2)}) async-start(), calls=%async_computation.13 | async-start | bytes 4718592 | tf_op jit(solution)/shard_map/reduce_scatter | solution.py:249
  174.1 26.4 %copy-start.13 = (bf16[3,80,1024]{2,1,0:T(8,128)(2,1)S(1)}, bf16[3,80,1024]{2,1,0:T(8,128)(2,1)}, u32[]{:S(2)}) copy-start(bf16[3,80,1024]{2,1,0:T(8,128)(2,1)} %param.17) | copy-start | bytes 1474564
  200.5 11.3 %copy-start.20 = (bf16[1024,4096]{1,0:T(8,128)(2,1)S(1)}, bf16[1024,4096]{1,0:T(8,128)(2,1)}, u32[]{:S(2)}) copy-start(bf16[1024,4096]{1,0:T(8,128)(2,1)} %all-gather.17.cloned.1.call-done) | copy-start | bytes 25165828
  224.9 18.9 %all-to-all-start.2 = ((bf16[4,2,30720]{2,1,0:T(2,128)(2,1)}), bf16[4,2,30720]{2,1,0:T(2,128)(2,1)}, u32[]{:S(2)}, u32[]{:S(2)}) async-start(bf16[4,2,30720]{2,1,0:T(2,128)(2,1)} %reshape.210), calls=%async_computation.2 | async-start | bytes 983040 | tf_op jit(solution)/shard_map/all_to_all | solution.py:213
  229.5 215.0 %reduce-scatter.5.cloned.1.call-start = ((), (), s32[]{:S(2)}) async-start(), calls=%async_computation.12 | async-start | bytes 14155776 | tf_op jit(solution)/shard_map/reduce_scatter | solution.py:247
  272.7 14.5 %copy-start.6 = (bf16[3,320,1,256]{3,2,0,1:T(2,128)(2,1)S(1)}, bf16[3,320,1,256]{3,2,0,1:T(2,128)(2,1)}, u32[]{:S(2)}) copy-start(bf16[3,320,1,256]{3,2,0,1:T(2,128)(2,1)} %copy.90) | copy-start | bytes 1474564
  353.8 210.7 %reduce-scatter.11.cloned.1.call-start = ((), (), s32[]{:S(2)}) async-start(), calls=%async_computation.15 | async-start | bytes 18874368 | tf_op jit(solution)/shard_map/reduce_scatter | solution.py:255
  368.6 315.8 %reduce-scatter.9.cloned.1.call-start = ((), (), s32[]{:S(2)}) async-start(), calls=%async_computation.14 | async-start | bytes 18874368 | tf_op jit(solution)/shard_map/reduce_scatter | solution.py:253
  378.9 432.2 %all-reduce.13.cloned.1.call-start = ((), (), s32[]{:S(2)}) async-start(), calls=%async_computation.16 | async-start | bytes 6291456 | tf_op jit(solution)/shard_map/psum | solution.py:262
  567.2 120.0 %copy-start.21 = (u32[32]{0:T(128)S(1)}, u32[32]{0:T(128)}, u32[]{:S(2)}) copy-start(u32[32]{0:T(128)} %constant.44) | copy-start | bytes 388
  567.2 122.5 %copy-start.19 = (bf16[128]{0:T(256)(128)(2,1)S(1)}, bf16[128]{0:T(256)(128)(2,1)}, u32[]{:S(2)}) copy-start(bf16[128]{0:T(256)(128)(2,1)} %param.29) | copy-start | bytes 772
  698.5 8.4 %copy-start.5 = (bf16[3,80,3072]{2,1,0:T(8,128)(2,1)S(1)}, bf16[3,80,3072]{2,1,0:T(8,128)(2,1)}, u32[]{:S(2)}) copy-start(bf16[3,80,3072]{2,1,0:T(8,128)(2,1)} %reshape.165) | copy-start | bytes 4423684
  706.9 47.9 %copy-start.4 = (bf16[3,80,1024]{2,1,0:T(8,128)(2,1)S(1)}, bf16[3,80,1024]{2,1,0:T(8,128)(2,1)}, u32[]{:S(2)}) copy-start(bf16[3,80,1024]{2,1,0:T(8,128)(2,1)} %param.15) | copy-start | bytes 1474564
  (10 other events, 45.0 us)
Sparse Core Ops, SparseCore 0:
  9.9 48.2 all-gather.12
  60.1 27.8 all-gather.14
  89.9 54.3 all-gather.16
  146.1 54.4 all-gather.18
  218.1 51.3 reduce-scatter.6
  353.9 90.5 reduce-scatter.4
  448.5 115.9 reduce-scatter.10
  568.5 115.9 reduce-scatter.8
  688.4 122.6 all-reduce.12
where the time goes:
time: 836 us; the launch traced here: 826 us
  waiting for transfers between devices  443 us (53%)
  blocking collectives  155 us (19%)
  matrix products  114 us (14%)
  local copies, waits for them, and re-layouts  52.6 us (6%)
  other arithmetic  31.7 us (4%)
  between operations  16.5 us (2%)
  starting transfers between devices  13.2 us (2%)
    reduce_scatter x1, waiting for transfers between devices, per_device(): lax.psum_scatter(down_gradient, 'fsdp', scatter_dimension=0, tiled=True)  118 us
    reduce_scatter x1, waiting for transfers between devices, per_device(): lax.psum_scatter(up_projection_gradient, 'fsdp', scatter_dimension=0, til...  117 us
    dot_general x18, matrix products, matrix_product(): return jnp.einsum(form, left, right, preferred_element_type=jnp.float32)  114 us
    reduce_scatter x1, waiting for transfers between devices, per_device(): lax.psum_scatter(query_key_value_weight_gradient, 'fsdp', scatter_dimensi...  63.7 us
    psum x1, waiting for transfers between devices, per_device(): lax.psum(shares[2].astype(jnp.bfloat16), 'seq').astype(jnp.float32)  55 us
    all_to_all x1, blocking collectives, per_device(): lax.all_to_all(stacked, 'seq', split_axis=1, concat_axis=3, tiled=True)  48.1 us
    all_to_all x1, waiting for transfers between devices, per_device(): lax.all_to_all(query_key_value_rows, 'seq', split_axis=3, concat_axis=1,...  35.3 us
    unnamed x1, blocking collectives  25.7 us
  transfers between devices with their start and end apart: 12, of which 8 were waited for; matrix products, arithmetic and copies ran while one was open for 20% of the time, Pallas kernels for 0%

commit v1 on v0

--- a/solution.py
+++ b/solution.py
@@ -122,7 +122,10 @@
         matrix_product("vgp,pf->vgf", normalized_reduced, query_key_value_weight) + complete_bias
     ).astype(jnp.bfloat16)
     query_key_value_rows = query_key_value_rows.reshape(seq_count, local_slots, 3, model_width)
-    heads = lax.all_to_all(query_key_value_rows, "seq", split_axis=3, concat_axis=1, tiled=True)
+    size = lax.axis_size("seq")
+    blocks = jnp.stack(jnp.split(query_key_value_rows, size, axis=3), axis=0)
+    blocks = lax.all_to_all(blocks, "seq", split_axis=0, concat_axis=0)
+    heads = jnp.concatenate(blocks, axis=1)
     queries = heads[:, :, 0].reshape(seq_count, all_slots, head_count, HEAD)
     key_rows = heads[:, :, 1].reshape(seq_count, all_slots, head_count, HEAD)
     value_rows = heads[:, :, 2].reshape(seq_count, all_slots, head_count, HEAD)

time: 836 us -> 837 us (level)
  local copies, waits for them, and re-layouts: 52.6 us -> 35.2 us
  waiting for transfers between devices: 443 us -> 456 us
    all_gather x1, waiting for transfers between devices: 18.3 us -> 34.3 us  [per_device(): lax.all_gather(shards[10], 'fsdp', axis=0, tiled=True)]
    unnamed x62 -> x90, local copies, waits for them, and re-layouts: 18 us -> 7.52 us
  transfers between devices with their start and end apart: 12 -> 12, of which waited for: 8 -> 8; matrix products, arithmetic and copies ran while one was open for 20% -> 19% of each run, Pallas kernels for 0% -> 0%
where the time goes in v1:
time: 837 us; the launch traced here: 828 us
  waiting for transfers between devices  456 us (54%)
  blocking collectives  155 us (19%)
  matrix products  117 us (14%)
  other arithmetic  35.6 us (4%)
  local copies, waits for them, and re-layouts  35.2 us (4%)
  between operations  16.6 us (2%)
  starting transfers between devices  13.2 us (2%)
    reduce_scatter x1, waiting for transfers between devices, per_device(): lax.psum_scatter(down_gradient, 'fsdp', scatter_dimension=0, tiled=True)  118 us
    reduce_scatter x1, waiting for transfers between devices, per_device(): lax.psum_scatter(up_projection_gradient, 'fsdp', scatter_dimension=0, til...  117 us
    dot_general x18, matrix products, matrix_product(): return jnp.einsum(form, left, right, preferred_element_type=jnp.float32)  117 us
    reduce_scatter x1, waiting for transfers between devices, per_device(): lax.psum_scatter(query_key_value_weight_gradient, 'fsdp', scatter_dimensi...  62.3 us
    psum x1, waiting for transfers between devices, per_device(): lax.psum(shares[2].astype(jnp.bfloat16), 'seq').astype(jnp.float32)  54.9 us
    all_to_all x1, blocking collectives, per_device(): lax.all_to_all(stacked, 'seq', split_axis=1, concat_axis=3, tiled=True)  47.9 us
    all_to_all x1, waiting for transfers between devices, per_device(): blocks = lax.all_to_all(blocks, 'seq', split_axis=0, concat_axis=0)  35.2 us
    all_gather x1, waiting for transfers between devices, per_device(): lax.all_gather(shards[10], 'fsdp', axis=0, tiled=True)  34.3 us
  transfers between devices with their start and end apart: 12, of which 8 were waited for; matrix products, arithmetic and copies ran while one was open for 19% of the time, Pallas kernels for 0%

profile of v1, /device:TPU:0, one launch (start us, length us, event | category | flops | bytes accessed | tf_op | source)
XLA Modules:
  0.0 828.4 jit_solution(4525579459065572688)
XLA Ops:
  10.6 10.3 %all-gather = bf16[8,1,128]{2,1,0:T(2,128)(2,1)S(1)} all-gather(bf16[1,1,128]{2,1,0:T(2,128)(2,1)} %bitcast.174), channel_id=1, replica_groups=mesh['fsdp'=8,'seq'=4] {'fsdp'}, dimensions={0}, use_global_device_ids=true | all-gather | bytes 2304 | tf_op jit(solution)/shard_map/all_gather | solution.py:101
  20.9 8.6 %all-gather.1 = bf16[8,1,128]{2,1,0:T(2,128)(2,1)S(1)} all-gather(bf16[1,1,128]{2,1,0:T(2,128)(2,1)} %bitcast.175), channel_id=1, replica_groups=mesh['fsdp'=8,'seq'=4] {'fsdp'}, dimensions={0}, use_global_device_ids=true | all-gather | bytes 2304 | tf_op jit(solution)/shard_map/all_gather | solution.py:102
  29.6 8.0 all-gather.2
  39.2 19.0 %all-gather.13.cloned.1.call-done = bf16[1024,3072]{1,0:T(8,128)(2,1)} async-done(((bf16[128,3072]{1,0:T(8,128)(2,1)}), bf16[1024,3072]{1,0:T(8,128)(2,1)}) %all-gather.13.cloned.1.call-update) | async-done | bytes 6291472 | tf_op jit(solution)/shard_map/all_gather | solution.py:103
  76.8 35.2 %all-to-all-done = bf16[4,3,80,3,256]{4,2,3,1,0:T(8,128)(2,1)S(1)} async-done(((bf16[4,3,80,3,256]{4,2,3,1,0:T(8,128)(2,1)}), bf16[4,3,80,3,256]{4,2,3,1,0:T(8,128)(2,1)S(1)}, u32[]{:S(2)}, u32[]{:S(2)}) %all-to-all-start) | async-done | bytes 1474592 | tf_op jit(solution)/shard_map/all_to_all | solution.py:127
  122.2 8.7 %all-gather.3 = bf16[8,1,128]{2,1,0:T(2,128)(2,1)S(1)} all-gather(bf16[1,1,128]{2,1,0:T(2,128)(2,1)S(1)} %bitcast.176), channel_id=1, replica_groups=mesh['fsdp'=8,'seq'=4] {'fsdp'}, dimensions={0}, use_global_device_ids=true | all-gather | bytes 2304 | tf_op jit(solution)/shard_map/all_gather | solution.py:106
  138.7 8.7 %all-gather.5 = bf16[8,1,128]{2,1,0:T(2,128)(2,1)S(1)} all-gather(bf16[1,1,128]{2,1,0:T(2,128)(2,1)S(1)} %bitcast.178), channel_id=1, replica_groups=mesh['fsdp'=8,'seq'=4] {'fsdp'}, dimensions={0}, use_global_device_ids=true | all-gather | bytes 2304 | tf_op jit(solution)/shard_map/all_gather | solution.py:108
  147.4 8.1 all-gather.6
  166.2 34.3 %all-gather.19.cloned.1.call-done = bf16[4096,1024]{1,0:T(8,128)(2,1)} async-done(((bf16[512,1024]{1,0:T(8,128)(2,1)}), bf16[4096,1024]{1,0:T(8,128)(2,1)}) %all-gather.19.cloned.1.call-update) | async-done | bytes 8388624 | tf_op jit(solution)/shard_map/all_gather | solution.py:111
  200.5 11.9 %convert_reduce_fusion = (f32[4096]{0:T(1024)}, bf16[3,80,4096]{2,1,0:T(8,128)(2,1)S(1)}) fusion(f32[3,80,4096]{2,1,0:T(8,128)} %fusion.15, bf16[4096,1024]{1,0:T(8,128)(2,1)} %all-gather.19.cloned.1.call-done, bf16[3,80,1024]{2,1,0:T(8,128)(2,1)S(1)} %copy-done.11, f32[3,80]{1,0:T(4,128)S(1)} %compare_convert_fusion), kind=kOutput, calls=%fused_computation.35 | convolution fusion | flops 2035625984 | bytes 14795712 | tf_op jit(solution)/shard_map/jeo,xo->jex/dot_general | solution.py:28
  231.0 12.6 %all-to-all-done.2 = bf16[4,2,30720]{2,1,0:T(2,128)(2,1)S(1)} async-done(((bf16[4,2,30720]{2,1,0:T(2,128)(2,1)}), bf16[4,2,30720]{2,1,0:T(2,128)(2,1)S(1)}, u32[]{:S(2)}, u32[]{:S(2)}) %all-to-all-start.2) | async-done | bytes 491552 | tf_op jit(solution)/shard_map/all_to_all | solution.py:216
  260.3 11.8 %fusion.65 = bf16[3,4,64,320]{3,2,1,0:T(8,128)(2,1)} fusion(bf16[3,320,4,64]{1,3,2,0:T(8,128)(2,1)} %bitcast.145, f32[3,4,320,320]{2,3,1,0:T(8,128)} %fusion.117, f32[3,4,320,320]{2,3,1,0:T(8,128)} %copy-done, f32[3,4,320]{2,1,0:T(4,128)} %log_add_fusion), kind=kOutput, calls=%fused_computation.62 | convolution fusion | flops 166137920 | bytes 10828800 | tf_op jit(solution)/shard_map/shqk,skhe->sqhe/dot_general | solution.py:28
  275.2 11.1 %fusion.68 = bf16[3,4,64,320]{3,2,1,0:T(8,128)(2,1)} fusion(bf16[3,320,4,64]{1,3,2,0:T(8,128)(2,1)S(1)} %bitcast.143, f32[3,4,320,320]{2,3,1,0:T(8,128)} %fusion.117, f32[3,4,320,320]{2,3,1,0:T(8,128)} %copy-done, f32[3,4,320]{2,1,0:T(4,128)} %log_add_fusion), kind=kOutput, calls=%fused_computation.63 | convolution fusion | flops 166137920 | bytes 10828800 | tf_op jit(solution)/shard_map/shqk,sqhe->skhe/dot_general | solution.py:28
  294.0 47.9 %all_to_all.53 = bf16[3,320,3,256]{3,2,0,1:T(4,128)(2,1)S(1)} all-to-all(bf16[3,320,3,256]{3,2,0,1:T(4,128)(2,1)S(1)} %pad_maximum_fusion.1), channel_id=1, replica_groups=mesh['fsdp'=8,'seq'=4] {'seq'}, dimensions={1} | all-to-all | bytes 2949120 | tf_op jit(solution)/shard_map/all_to_all | solution.py:228
  356.5 15.1 %convolution_bitcast_fusion = f32[4096,1024]{1,0:T(8,128)} fusion(bf16[3,80,1024]{2,1,0:T(8,128)(2,1)} %param.17, f32[3,80]{1,0:T(4,128)S(1)} %copy-done.26, f32[3,80,4096]{2,1,0:T(8,128)} %fusion.15), kind=kOutput, calls=%fused_computation.1 | convolution fusion | flops 2022850560 | bytes 21201856 | tf_op jit(solution)/shard_map/zmx,zma->xa/dot_general | solution.py:28
  372.3 9.9 %convolution_bitcast_fusion.1 = f32[1024,4096]{1,0:T(8,128)} fusion(bf16[3,80,4096]{2,1,0:T(8,128)(2,1)} %copy-done.9, f32[3,80,1024]{2,1,0:T(8,128)S(1)} %get-tuple-element.59, f32[1024]{0:T(1024)S(1)} %bitcast.160, f32[1024]{0:T(1024)S(1)} %bitcast.158, f32[3,80]{1,0:T(4,128)S(1)} %copy-done.17, f32[3,80]{1,0:T(4,128)S(1)} %copy-done.13), kind=kOutput, calls=%fused_computation.2 | convolution fusion | flops 2014494720 | bytes 19736448 | tf_op jit(solution)/shard_map/znb,zng->bg/dot_general | solution.py:28
  384.2 62.3 %reduce-scatter.5.cloned.1.call-done = f32[128,3072]{1,0:T(8,128)} async-done(((f32[1024,3072]{1,0:T(8,128)}), f32[128,3072]{1,0:T(8,128)}) %reduce-scatter.5.cloned.1.call-update) | async-done | bytes 1572880 | tf_op jit(solution)/shard_map/reduce_scatter | solution.py:250
  448.9 117.6 %reduce-scatter.11.cloned.1.call-done = f32[512,1024]{1,0:T(8,128)} async-done(((f32[4096,1024]{1,0:T(8,128)}), f32[512,1024]{1,0:T(8,128)}) %reduce-scatter.11.cloned.1.call-update) | async-done | bytes 2097168 | tf_op jit(solution)/shard_map/reduce_scatter | solution.py:258
  569.2 117.2 %reduce-scatter.9.cloned.1.call-done = f32[128,4096]{1,0:T(8,128)} async-done(((f32[1024,4096]{1,0:T(8,128)}), f32[128,4096]{1,0:T(8,128)}) %reduce-scatter.9.cloned.1.call-update) | async-done | bytes 2097168 | tf_op jit(solution)/shard_map/reduce_scatter | solution.py:256
  691.7 8.8 %all-gather.7 = bf16[8,1,128]{2,1,0:T(2,128)(2,1)S(1)} all-gather(bf16[1,1,128]{2,1,0:T(2,128)(2,1)S(1)} %bitcast.179), channel_id=1, replica_groups=mesh['fsdp'=8,'seq'=4] {'fsdp'}, dimensions={0}, use_global_device_ids=true | all-gather | bytes 2304 | tf_op jit(solution)/shard_map/all_gather | solution.py:112
  700.5 8.1 fusion.80
  714.1 25.7 %all-reduce.8 = (bf16[1024]{0:T(1024)(128)(2,1)S(1)}, bf16[1024]{0:T(1024)(128)(2,1)S(1)}, bf16[2048]{0:T(1024)(128)(2,1)S(1)}, bf16[1024]{0:T(1024)(128)(2,1)S(...) all-reduce(f32[1024]{0:T(1024)S(1)} %get-tuple-element.16, ...), channel_id=2, replica_groups=mesh['fsdp'=8,'seq'=4] {'fsdp'}, use_global_device_ids=true, to_apply=%region_12.13.clone | all-reduce | flops 12288 | bytes 73728
  740.3 12.4 %all-reduce.9 = (bf16[128]{0:T(256)(128)(2,1)S(1)}, bf16[128]{0:T(256)(128)(2,1)S(1)}, bf16[256]{0:T(256)(128)(2,1)S(1)}, bf16[128]{0:T(256)(128)(2,1)S(1)}, bf1...) all-reduce(bf16[128]{0:T(256)(128)(2,1)S(1)} %dynamic-slice.31, ...), channel_id=1, replica_groups=mesh['fsdp'=8,'seq'=4] {'seq'}, use_global_device_ids=true, to_apply=%region_13.14 | all-reduce | flops 1536 | bytes 6144 | tf_op jit(solution)/shard_map/psum | solution.py:263
  758.1 54.9 %all-reduce.13.cloned.1.call-done = (bf16[128,3072]{1,0:T(8,128)(2,1)}, bf16[128,1024]{1,0:T(8,128)(2,1)}, bf16[128,4096]{1,0:T(8,128)(2,1)}, bf16[512,1024]{1,0:T(8,128)(2,1)}) async-done(((bf16[128,3072]{1,0:T(8,128)(2,1)}, bf16[128,1024]{1,0:T(8,128)(2,1)}, bf16[128,4096]{1,0:T(8,128)(2,1)}, bf16[512,1024]{1,0:T(8,128)(2,1)}), (bf16[128,3072]{1,0:T(8,128)(2,1)}, bf16[128,1024]{1,0:T(8,128)(2,1)}, ...) | async-done | bytes 3145744 | tf_op jit(solution)/shard_map/psum | solution.py:265
  (195 shorter events, 143.5 us)
Async XLA Ops:
  7.2 31.7 %copy-start.1 = (bf16[3,80,1024]{2,1,0:T(8,128)(2,1)S(1)}, bf16[3,80,1024]{2,1,0:T(8,128)(2,1)}, u32[]{:S(2)}) copy-start(bf16[3,80,1024]{2,1,0:T(8,128)(2,1)} %param.15) | copy-start | bytes 1474564
  7.2 51.0 %all-gather.13.cloned.1.call-start = ((), (), s32[]{:S(2)}) async-start(), calls=%async_computation.8 | async-start | bytes 7077888 | tf_op jit(solution)/shard_map/all_gather | solution.py:103
  7.9 147.8 %all-gather.15.cloned.1.call-start = ((), (), s32[]{:S(2)}) async-start(), calls=%async_computation.9 | async-start | bytes 2359296 | tf_op jit(solution)/shard_map/all_gather | solution.py:105
  8.7 149.8 %all-gather.17.cloned.1.call-start = ((), (), s32[]{:S(2)}) async-start(), calls=%async_computation.10 | async-start | bytes 9437184 | tf_op jit(solution)/shard_map/all_gather | solution.py:109
  9.4 191.1 %all-gather.19.cloned.1.call-start = ((), (), s32[]{:S(2)}) async-start(), calls=%async_computation.11 | async-start | bytes 9437184 | tf_op jit(solution)/shard_map/all_gather | solution.py:111
  38.9 19.3 %copy-start.18 = (f32[3,80]{1,0:T(4,128)}, f32[3,80]{1,0:T(4,128)S(1)}, u32[]{:S(2)}) copy-start(f32[3,80]{1,0:T(4,128)S(1)} %broadcast_multiply_fusion.5) | copy-start | bytes 2884
  39.2 19.0 %copy-start.20 = (f32[3,80]{1,0:T(4,128)}, f32[3,80]{1,0:T(4,128)S(1)}, u32[]{:S(2)}) copy-start(f32[3,80]{1,0:T(4,128)S(1)} %add_rsqrt_fusion.1) | copy-start | bytes 2884
  72.2 39.9 %all-to-all-start = ((bf16[4,3,80,3,256]{4,2,3,1,0:T(8,128)(2,1)}), bf16[4,3,80,3,256]{4,2,3,1,0:T(8,128)(2,1)S(1)}, u32[]{:S(2)}, u32[]{:S(2)}) async-start(bf16[4,3,80,3,256]{4,2,3,1,0:T(8,128)(2,1)} %copy.51), calls=%async_computation | async-start | bytes 2949120 | tf_op jit(solution)/shard_map/all_to_all | solution.py:127
  115.8 22.9 %copy-start.33 = (bf16[128]{0:T(256)(128)(2,1)S(1)}, bf16[128]{0:T(256)(128)(2,1)}, u32[]{:S(2)}) copy-start(bf16[128]{0:T(256)(128)(2,1)} %param.25) | copy-start | bytes 772
  118.6 37.0 %all-to-all-start.1 = ((bf16[3,320,256]{2,0,1:T(4,128)(2,1)}), bf16[3,320,256]{2,0,1:T(4,128)(2,1)S(1)}, u32[]{:S(2)}, u32[]{:S(2)}) async-start(bf16[3,320,256]{2,0,1:T(4,128)(2,1)} %copy.57), calls=%async_computation.1 | async-start | bytes 1310720 | tf_op jit(solution)/shard_map/all_to_all | solution.py:142
  122.1 260.2 %reduce-scatter.7.cloned.1.call-start = ((), (), s32[]{:S(2)}) async-start(), calls=%async_computation.13 | async-start | bytes 4718592 | tf_op jit(solution)/shard_map/reduce_scatter | solution.py:252
  155.6 60.0 %copy-start.25 = (f32[3,80]{1,0:T(4,128)}, f32[3,80]{1,0:T(4,128)S(1)}, u32[]{:S(2)}) copy-start(f32[3,80]{1,0:T(4,128)S(1)} %compare_convert_fusion) | copy-start | bytes 2884
  158.2 57.5 %copy-start.12 = (f32[3,80]{1,0:T(4,128)}, f32[3,80]{1,0:T(4,128)S(1)}, u32[]{:S(2)}) copy-start(f32[3,80]{1,0:T(4,128)S(1)} %broadcast_multiply_fusion.4) | copy-start | bytes 2884
  158.4 57.2 %copy-start.16 = (f32[3,80]{1,0:T(4,128)}, f32[3,80]{1,0:T(4,128)S(1)}, u32[]{:S(2)}) copy-start(f32[3,80]{1,0:T(4,128)S(1)} %add_rsqrt_fusion) | copy-start | bytes 2884
  158.5 42.0 %copy-start.11 = (bf16[3,80,1024]{2,1,0:T(8,128)(2,1)S(1)}, bf16[3,80,1024]{2,1,0:T(8,128)(2,1)}, u32[]{:S(2)}) copy-start(bf16[3,80,1024]{2,1,0:T(8,128)(2,1)} %param.17) | copy-start | bytes 1474564
  224.8 18.8 %all-to-all-start.2 = ((bf16[4,2,30720]{2,1,0:T(2,128)(2,1)}), bf16[4,2,30720]{2,1,0:T(2,128)(2,1)S(1)}, u32[]{:S(2)}, u32[]{:S(2)}) async-start(bf16[4,2,30720]{2,1,0:T(2,128)(2,1)} %reshape.216), calls=%async_computation.2 | async-start | bytes 983040 | tf_op jit(solution)/shard_map/all_to_all | solution.py:216
  229.4 217.1 %reduce-scatter.5.cloned.1.call-start = ((), (), s32[]{:S(2)}) async-start(), calls=%async_computation.12 | async-start | bytes 14155776 | tf_op jit(solution)/shard_map/reduce_scatter | solution.py:250
  231.0 17.8 %copy-start.15 = (f32[3,4,320]{2,1,0:T(4,128)S(1)}, f32[3,4,320]{2,1,0:T(4,128)}, u32[]{:S(2)}) copy-start(f32[3,4,320]{2,1,0:T(4,128)} %log_add_fusion) | copy-start | bytes 46084
  355.8 210.6 %reduce-scatter.11.cloned.1.call-start = ((), (), s32[]{:S(2)}) async-start(), calls=%async_computation.15 | async-start | bytes 18874368 | tf_op jit(solution)/shard_map/reduce_scatter | solution.py:258
  371.6 314.8 %reduce-scatter.9.cloned.1.call-start = ((), (), s32[]{:S(2)}) async-start(), calls=%async_computation.14 | async-start | bytes 18874368 | tf_op jit(solution)/shard_map/reduce_scatter | solution.py:256
  382.2 430.8 %all-reduce.13.cloned.1.call-start = ((), (), s32[]{:S(2)}) async-start(), calls=%async_computation.16 | async-start | bytes 6291456 | tf_op jit(solution)/shard_map/psum | solution.py:265
  569.2 120.0 %copy-start.36 = (u32[32]{0:T(128)S(1)}, u32[32]{0:T(128)}, u32[]{:S(2)}) copy-start(u32[32]{0:T(128)} %constant.44) | copy-start | bytes 388
  569.2 122.5 %copy-start.34 = (bf16[128]{0:T(256)(128)(2,1)S(1)}, bf16[128]{0:T(256)(128)(2,1)}, u32[]{:S(2)}) copy-start(bf16[128]{0:T(256)(128)(2,1)} %param.29) | copy-start | bytes 772
  708.9 48.0 %copy-start.3 = (bf16[3,80,1024]{2,1,0:T(8,128)(2,1)S(1)}, bf16[3,80,1024]{2,1,0:T(8,128)(2,1)}, u32[]{:S(2)}) copy-start(bf16[3,80,1024]{2,1,0:T(8,128)(2,1)} %param.15) | copy-start | bytes 1474564
  (25 other events, 138.5 us)
Sparse Core Ops, SparseCore 0:
  9.9 48.2 all-gather.12
  60.1 27.8 all-gather.14
  89.9 54.3 all-gather.16
  146.1 54.3 all-gather.18
  219.7 51.3 reduce-scatter.6
  355.9 90.5 reduce-scatter.4
  450.5 115.9 reduce-scatter.10
  570.4 115.9 reduce-scatter.8
  690.4 122.5 all-reduce.12
